TPU v7x, 512 devices: a whole 4x4x16 slice. The times are simulated.
512 devices in a mesh: tp: 16 (over z_hi, y, core), dp: 32 (over z_lo, x).
Axes of the slice: x: 4, y: 4, z: 16 (z_hi: 2, z_lo: 8; z = z_hi * 8 + z_lo), core: 2. Of those that a mesh axis runs over, the one named last changes fastest.
Arguments:
- tokens: bfloat16 [2048, 4096], P(('tp', 'dp')), may hold values from -6 to 6
- norm_gain: float32 [4096], replicated, may hold values from 0.1 to 1.9
- gate_slots: bfloat16 [1536, 128, 128], P(('tp', 'dp')), may hold values from -0.1875 to 0.1875
- up_slots: bfloat16 [1536, 128, 128], P(('tp', 'dp')), may hold values from -0.1875 to 0.1875
- down_slots: bfloat16 [1536, 128, 128], P(('tp', 'dp')), may hold values from -0.09375 to 0.09375
- gate_ids: int32 [1536], P('tp'), may hold values from -1 to 223, as said below
- up_ids: int32 [1536], P('tp'), may hold values from -1 to 223, as said below
- down_ids: int32 [1536], P('tp'), may hold values from -1 to 223, as said below
Outputs:
- mixed: bfloat16 [2048, 4096], P(('tp', 'dp'))
Inputs may be any that keep to these rules, and one draw needn't show every extreme that they name: `gate_ids`: each entry is -1 (an empty slot) or a block number j * 32 + k, j a hidden block of that tp index and k a block of the model width. The live numbers of one tp index are distinct and stand in its first slots; each tp index keeps at most 96 blocks, and one tp index keeps exactly 96. `up_ids`: as for gate_ids, drawn independently. `down_ids`: as for gate_ids, drawn independently.
All inputs are finite; a program needn't handle non-finite values.
Results may differ from a plain program's by a relative error of at most 0.015.
Values may be sent and summed in bfloat16 or wider, within the bound.
A program may use at most 128 MiB of HBM per device.

v0:
```python
import jax
import jax.numpy as jnp
from jax import lax
from jax.sharding import PartitionSpec as P

FF = 14336
EPSILON = 1e-05


def normalize(tokens, norm_gain):
    values = tokens.astype(jnp.float32)
    meansq = jnp.mean(values * values, axis=-1, keepdims=True)
    return (values * lax.rsqrt(meansq + EPSILON) * norm_gain).astype(jnp.bfloat16)


def decode(slot_ids, kblocks):
    slot_live = slot_ids >= 0
    hidden_block = jnp.where(slot_live, slot_ids // kblocks, 0)
    depth_block = jnp.where(slot_live, slot_ids % kblocks, 0)
    return (hidden_block, depth_block, slot_live)


def block_terms(inputs, slot_values, source, target, slot_live, width_in, width_out):
    block_side = slot_values.shape[1]
    rows_count = inputs.shape[0]
    blocked = inputs.reshape(rows_count, width_in, block_side)
    picked = jnp.take(blocked, source, axis=1)
    products = jnp.einsum("rca,cab->rcb", picked, slot_values, preferred_element_type=jnp.float32)
    placing = ((target[:, None] == jnp.arange(width_out)[None, :]) & slot_live[:, None]).astype(
        jnp.bfloat16
    )
    upper = products.astype(jnp.bfloat16)
    lower = (products - upper.astype(jnp.float32)).astype(jnp.bfloat16)
    summed = jnp.einsum("rcb,cn->rnb", upper, placing, preferred_element_type=jnp.float32)
    summed = summed + jnp.einsum("rcb,cn->rnb", lower, placing, preferred_element_type=jnp.float32)
    return summed.reshape(rows_count, width_out * block_side)


def shards(tokens, norm_gain, gate_slots, up_slots, down_slots, gate_ids, up_ids, down_ids):
    block_side = gate_slots.shape[1]
    model_width = tokens.shape[1]
    kblocks = model_width // block_side
    hblocks = FF // (block_side * lax.axis_size("tp"))
    normed = normalize(tokens, norm_gain)
    gathered = lax.all_gather(normed, "tp", axis=0, tiled=True)
    gate_hidden, gate_depth, gate_live = decode(gate_ids, kblocks)
    up_hidden, up_depth, up_live = decode(up_ids, kblocks)
    down_hidden, down_depth, down_live = decode(down_ids, kblocks)
    all_gate, all_up, all_down = (
        lax.all_gather(gate_slots, "dp", axis=0, tiled=True),
        lax.all_gather(up_slots, "dp", axis=0, tiled=True),
        lax.all_gather(down_slots, "dp", axis=0, tiled=True),
    )
    gate_act = block_terms(gathered, all_gate, gate_depth, gate_hidden, gate_live, kblocks, hblocks)
    up_act = block_terms(gathered, all_up, up_depth, up_hidden, up_live, kblocks, hblocks)
    hidden = (jax.nn.silu(gate_act) * up_act).astype(jnp.bfloat16)
    partial_value = block_terms(
        hidden, all_down, down_hidden, down_depth, down_live, hblocks, kblocks
    )
    branch_sum = lax.psum_scatter(
        partial_value.astype(jnp.bfloat16), "tp", scatter_dimension=0, tiled=True
    ).astype(jnp.float32)
    return (tokens.astype(jnp.float32) + branch_sum).astype(jnp.bfloat16)


def solution(mesh):
    placed = (
        P(("tp", "dp"), None),
        P(),
        P(("tp", "dp"), None, None),
        P(("tp", "dp"), None, None),
        P(("tp", "dp"), None, None),
        P("tp"),
        P("tp"),
        P("tp"),
    )
    return jax.shard_map(
        shards, mesh=mesh, in_specs=placed, out_specs=P(("tp", "dp"), None), check_vma=False
    )
```

profile of v0, /device:TPU:1, one launch (start us, length us, event | category | flops | bytes accessed | tf_op | source)
XLA Modules:
  0.0 964.0 jit_solution(2715450965105830085)
XLA Ops:
  6.5 0.0 copy-start.1
  6.5 0.0 all-gather.5.cloned.1.call-start
  6.5 0.7 all-gather.5.cloned.1.call-update
  7.3 0.0 all-gather.7.cloned.1.call-start
  7.3 0.7 all-gather.7.cloned.1.call-update
  8.0 0.0 all-gather.9.cloned.1.call-start
  8.1 0.7 all-gather.9.cloned.1.call-update
  8.7 0.0 all-reduce.3.cloned.1.call-start
  8.8 0.9 fusion.54
  9.7 0.9 fusion.58
  10.6 55.3 %all-gather = bf16[16,4,4096]{2,1,0:T(4,128)(2,1)S(1)} all-gather(bf16[1,4,4096]{2,1,0:T(4,128)(2,1)S(1)} %fusion.58), channel_id=1, replica_groups=mesh['tp'=16,'dp'=32] {'tp'}, dimensions={0}, use_global_device_ids=true | all-gather | bytes 557056 | tf_op jit(solution)/shard_map/all_gather | solution.py:45
  65.8 0.5 reshape.34
  66.4 0.2 copy.28
  66.6 0.0 copy-done.1
  66.6 0.0 copy-start.2
  66.6 1.9 gather_fusion.1
  68.6 0.0 copy-done.2
  68.6 0.0 copy-start.3
  68.6 0.8 gather_fusion.2
  69.5 0.0 copy-done.3
  69.6 152.0 %all-gather.5.cloned.1.call-done = bf16[96,128,128]{2,1,0:T(8,128)(2,1)} async-done(((bf16[3,128,128]{2,1,0:T(8,128)(2,1)}), bf16[96,128,128]{2,1,0:T(8,128)(2,1)}) %all-gather.5.cloned.1.call-update) | async-done | bytes 3145744 | tf_op jit(solution)/shard_map/all_gather | solution.py:50
  221.5 3.4 fusion.2
  224.9 0.9 fusion.17
  225.8 222.5 %all-gather.7.cloned.1.call-done = bf16[96,128,128]{2,1,0:T(8,128)(2,1)} async-done(((bf16[3,128,128]{2,1,0:T(8,128)(2,1)}), bf16[96,128,128]{2,1,0:T(8,128)(2,1)}) %all-gather.7.cloned.1.call-update) | async-done | bytes 3145744 | tf_op jit(solution)/shard_map/all_gather | solution.py:51
  448.3 2.9 fusion.1
  451.2 0.9 fusion.13
  452.2 0.9 fusion.36
  453.1 1.0 fusion.48
  454.1 0.8 gather_fusion
  455.0 219.7 %all-gather.9.cloned.1.call-done = bf16[96,128,128]{2,1,0:T(8,128)(2,1)} async-done(((bf16[3,128,128]{2,1,0:T(8,128)(2,1)}), bf16[96,128,128]{2,1,0:T(8,128)(2,1)}) %all-gather.9.cloned.1.call-update) | async-done | bytes 3145744 | tf_op jit(solution)/shard_map/all_gather | solution.py:52
  674.7 2.9 fusion
  677.6 1.0 fusion.9
  678.6 1.1 fusion.30
  679.7 0.0 copy-start
  679.7 1.0 copy.67
  680.7 0.0 all-reduce.3.cloned.1.call-update
  680.8 1.3 dynamic-slice
  682.7 273.2 %all-reduce.3.cloned.1.call-done = bf16[64,4096]{1,0:T(8,128)(2,1)} async-done(((bf16[64,4096]{1,0:T(8,128)(2,1)}), bf16[64,4096]{1,0:T(8,128)(2,1)}) %all-reduce.3.cloned.1.call-update) | async-done | bytes 524304
  955.9 0.0 copy-done
  955.9 1.5 fusion.57
  (11 shorter events, 0.1 us)
Async XLA Ops:
  6.5 60.1 %copy-start.1 = (s32[96]{0:T(128)S(1)}, s32[96]{0:T(128)}, u32[]{:S(2)}) copy-start(s32[96]{0:T(128)} %param.15) | copy-start | bytes 1156
  6.5 215.0 %all-gather.5.cloned.1.call-start = ((), (), s32[]{:S(2)}) async-start(), calls=%async_computation | async-start | bytes 3244032 | tf_op jit(solution)/shard_map/all_gather | solution.py:50
  7.3 441.1 %all-gather.7.cloned.1.call-start = ((), (), s32[]{:S(2)}) async-start(), calls=%async_computation.1 | async-start | bytes 3244032 | tf_op jit(solution)/shard_map/all_gather | solution.py:51
  8.0 666.7 %all-gather.9.cloned.1.call-start = ((), (), s32[]{:S(2)}) async-start(), calls=%async_computation.2 | async-start | bytes 3244032 | tf_op jit(solution)/shard_map/all_gather | solution.py:52
  8.7 947.2 %all-reduce.3.cloned.1.call-start = ((), (), s32[]{:S(2)}) async-start(), calls=%async_computation.3 | async-start | bytes 1048576
  66.6 2.0 copy-start.2
  68.6 0.9 copy-start.3
  679.7 276.2 %copy-start = (bf16[4,4096]{1,0:T(4,128)(2,1)S(1)}, bf16[4,4096]{1,0:T(4,128)(2,1)}, u32[]{:S(2)}) copy-start(bf16[4,4096]{1,0:T(4,128)(2,1)} %param.10) | copy-start | bytes 98308
Sparse Core Ops, SparseCore 0:
  9.4 212.0 all-gather.4
  223.6 224.6 all-gather.6
  450.4 224.2 all-gather.8
  680.9 275.0 all-reduce.2
where the time goes:
time: 964 us
  waiting for transfers between devices  869 us (90%)
  blocking collectives  55.3 us (6%)
  matrix products  15.1 us (2%)
  between operations  13.9 us (1%)
    unnamed x5, waiting for transfers between devices  275 us
    all_gather x1, waiting for transfers between devices, shards(): lax.all_gather(up_slots, 'dp', axis=0, tiled=True)  222 us
    all_gather x1, waiting for transfers between devices, shards(): lax.all_gather(down_slots, 'dp', axis=0, tiled=True)  220 us
    all_gather x1, waiting for transfers between devices, shards(): lax.all_gather(gate_slots, 'dp', axis=0, tiled=True)  152 us
    all_gather x1, blocking collectives, shards(): gathered = lax.all_gather(normed, 'tp', axis=0, tiled=True)  55.3 us
  transfers between devices with their start and end apart: 4, of which 4 were waited for; matrix products, arithmetic and copies ran while one was open for 2% of the time, Pallas kernels for 0%

commit v1 on v0

--- a/solution.py
+++ b/solution.py
@@ -48,7 +48,9 @@
     down_hidden, down_depth, down_live = decode(down_ids, kblocks)
     all_gate, all_up, all_down = (
         lax.all_gather(gate_slots, "dp", axis=0, tiled=True),
-        lax.all_gather(up_slots, "dp", axis=0, tiled=True),
+        jnp.concatenate(
+            lax.all_to_all(jnp.stack([up_slots] * lax.axis_size("dp")), "dp", 0, 0), axis=0
+        ),
         lax.all_gather(down_slots, "dp", axis=0, tiled=True),
     )
     gate_act = block_terms(gathered, all_gate, gate_depth, gate_hidden, gate_live, kblocks, hblocks)

time: 964 us -> 754 us (0.78)
  waiting for transfers between devices: 869 us -> 595 us
  blocking collectives: 55.3 us -> 102 us
  starting transfers between devices: 0.12 us -> 16.3 us
    all_gather x1 -> x0, waiting for transfers between devices: 222 us -> none  [shards(): lax.all_gather(up_slots, 'dp', axis=0, tiled=True)]
    all_gather x1, blocking collectives: 55.3 us -> 102 us  [shards(): gathered = lax.all_gather(normed, 'tp', axis=0, tiled=True)]
    all_gather x1, waiting for transfers between devices: 152 us -> 106 us  [shards(): lax.all_gather(gate_slots, 'dp', axis=0, tiled=True)]
    all_to_all x0 -> x1, starting transfers between devices: none -> 16.2 us  [shards(): lax.all_to_all(jnp.stack([up_slots] * lax.axis_size('dp')), 'dp', 0, 0)]
    unnamed x5 -> x4, waiting for transfers between devices: 275 us -> 275 us
  transfers between devices with their start and end apart: 4 -> 4, of which waited for: 4 -> 3; matrix products, arithmetic and copies ran while one was open for 2% -> 2% of each run, Pallas kernels for 0% -> 0%
where the time goes in v1:
time: 754 us
  waiting for transfers between devices  595 us (79%)
  blocking collectives  102 us (14%)
  starting transfers between devices  16.3 us (2%)
  matrix products  15.1 us (2%)
  between operations  14 us (2%)
  local copies, waits for them, and re-layouts  10.1 us (1%)
    unnamed x4, waiting for transfers between devices  275 us
    all_gather x1, waiting for transfers between devices, shards(): lax.all_gather(down_slots, 'dp', axis=0, tiled=True)  214 us
    all_gather x1, waiting for transfers between devices, shards(): lax.all_gather(gate_slots, 'dp', axis=0, tiled=True)  106 us
    all_gather x1, blocking collectives, shards(): gathered = lax.all_gather(normed, 'tp', axis=0, tiled=True)  102 us
    all_to_all x1, starting transfers between devices, shards(): lax.all_to_all(jnp.stack([up_slots] * lax.axis_size('dp')), 'dp', 0, 0)  16.2 us
  transfers between devices with their start and end apart: 4, of which 3 were waited for; matrix products, arithmetic and copies ran while one was open for 2% of the time, Pallas kernels for 0%

profile of v1, /device:TPU:1, one launch (start us, length us, event | category | flops | bytes accessed | tf_op | source)
XLA Modules:
  0.0 753.9 jit_solution(8165946056005531833)
XLA Ops:
  6.5 3.4 stack.2
  9.9 0.0 copy-start
  9.9 0.0 copy-start.1
  9.9 16.2 %all-to-all-start = ((bf16[32,3,128,128]{3,2,1,0:T(8,128)(2,1)}), bf16[32,3,128,128]{3,2,1,0:T(8,128)(2,1)}, u32[]{:S(2)}, u32[]{:S(2)}) async-start(bf16[32,3,128,128]{3,2,1,0:T(8,128)(2,1)} %stack.2), calls=%async_computation | async-start | bytes 6291456 | tf_op jit(solution)/shard_map/all_to_all | solution.py:52
  26.1 0.0 copy-start.2
  26.1 0.0 all-gather.4.cloned.1.call-start
  26.1 0.7 all-gather.4.cloned.1.call-update
  26.8 0.0 all-gather.6.cloned.1.call-start
  26.9 0.7 all-gather.6.cloned.1.call-update
  27.6 0.0 all-reduce.3.cloned.1.call-start
  27.6 0.0 copy-done
  27.6 0.1 fusion.54
  27.8 0.0 copy-done.1
  27.8 0.1 fusion.58
  27.9 102.0 %all-gather = bf16[16,4,4096]{2,1,0:T(4,128)(2,1)S(1)} all-gather(bf16[1,4,4096]{2,1,0:T(4,128)(2,1)S(1)} %fusion.58), channel_id=1, replica_groups=mesh['tp'=16,'dp'=32] {'tp'}, dimensions={0}, use_global_device_ids=true | all-gather | bytes 557056 | tf_op jit(solution)/shard_map/all_gather | solution.py:45
  129.9 0.5 reshape.39
  130.4 0.2 copy.28
  130.6 0.0 copy-done.2
  130.7 0.0 copy-start.3
  130.7 2.0 gather_fusion.1
  132.7 0.0 copy-done.3
  132.7 0.0 copy-start.4
  132.7 0.8 gather_fusion.2
  133.6 0.0 copy-done.4
  133.7 106.0 %all-gather.4.cloned.1.call-done = bf16[96,128,128]{2,1,0:T(8,128)(2,1)} async-done(((bf16[3,128,128]{2,1,0:T(8,128)(2,1)}), bf16[96,128,128]{2,1,0:T(8,128)(2,1)}) %all-gather.4.cloned.1.call-update) | async-done | bytes 3145744 | tf_op jit(solution)/shard_map/all_gather | solution.py:50
  239.7 3.4 fusion.2
  243.1 0.9 fusion.17
  244.0 0.9 fusion.36
  245.0 0.0 all-to-all-done
  245.0 2.9 fusion.1
  247.9 0.9 fusion.13
  248.8 1.0 fusion.48
  249.8 0.8 gather_fusion
  250.7 213.9 %all-gather.6.cloned.1.call-done = bf16[96,128,128]{2,1,0:T(8,128)(2,1)} async-done(((bf16[3,128,128]{2,1,0:T(8,128)(2,1)}), bf16[96,128,128]{2,1,0:T(8,128)(2,1)}) %all-gather.6.cloned.1.call-update) | async-done | bytes 3145744 | tf_op jit(solution)/shard_map/all_gather | solution.py:54
  464.6 2.9 fusion
  467.5 1.0 fusion.9
  468.6 1.1 fusion.30
  469.7 1.0 copy.67
  470.7 0.0 all-reduce.3.cloned.1.call-update
  470.7 1.3 dynamic-slice
  472.6 273.2 %all-reduce.3.cloned.1.call-done = bf16[64,4096]{1,0:T(8,128)(2,1)} async-done(((bf16[64,4096]{1,0:T(8,128)(2,1)}), bf16[64,4096]{1,0:T(8,128)(2,1)}) %all-reduce.3.cloned.1.call-update) | async-done | bytes 524304
  745.9 1.5 fusion.57
  (11 shorter events, 0.1 us)
Async XLA Ops:
  9.9 17.7 %copy-start = (bf16[4,4096]{1,0:T(4,128)(2,1)S(1)}, bf16[4,4096]{1,0:T(4,128)(2,1)}, u32[]{:S(2)}) copy-start(bf16[4,4096]{1,0:T(4,128)(2,1)} %param.10) | copy-start | bytes 98308
  9.9 17.9 %copy-start.1 = (f32[4096]{0:T(1024)S(1)}, f32[4096]{0:T(1024)}, u32[]{:S(2)}) copy-start(f32[4096]{0:T(1024)} %param.11) | copy-start | bytes 49156
  9.9 235.1 %all-to-all-start = ((bf16[32,3,128,128]{3,2,1,0:T(8,128)(2,1)}), bf16[32,3,128,128]{3,2,1,0:T(8,128)(2,1)}, u32[]{:S(2)}, u32[]{:S(2)}) async-start(bf16[32,3,128,128]{3,2,1,0:T(8,128)(2,1)} %stack.2), calls=%async_computation | async-start | bytes 6291456 | tf_op jit(solution)/shard_map/all_to_all | solution.py:52
  26.1 104.6 %copy-start.2 = (s32[96]{0:T(128)S(1)}, s32[96]{0:T(128)}, u32[]{:S(2)}) copy-start(s32[96]{0:T(128)} %param.15) | copy-start | bytes 1156
  26.1 213.6 %all-gather.4.cloned.1.call-start = ((), (), s32[]{:S(2)}) async-start(), calls=%async_computation.1 | async-start | bytes 3244032 | tf_op jit(solution)/shard_map/all_gather | solution.py:50
  26.8 437.8 %all-gather.6.cloned.1.call-start = ((), (), s32[]{:S(2)}) async-start(), calls=%async_computation.2 | async-start | bytes 3244032 | tf_op jit(solution)/shard_map/all_gather | solution.py:54
  27.6 718.3 %all-reduce.3.cloned.1.call-start = ((), (), s32[]{:S(2)}) async-start(), calls=%async_computation.3 | async-start | bytes 1048576
  130.7 2.0 copy-start.3
  132.7 0.9 copy-start.4
Sparse Core Ops, SparseCore 0:
  29.0 210.6 all-gather.3
  241.8 222.7 all-gather.5
  470.8 275.0 all-reduce.2
